TPU v7x, 128 devices: a whole 4x4x4 slice. The times are simulated.
128 devices in a mesh: blk: 32 (over x, z, y_lo), group: 4 (over y_hi, core).
Axes of the slice: x: 4, y: 4 (y_hi: 2, y_lo: 2; y = y_hi * 2 + y_lo), z: 4, core: 2. Of those that a mesh axis runs over, the one named last changes fastest.
Arguments:
- queries: bfloat16 [32, 2048, 2560], P('blk', 'group'), may hold values from -6 to 6
- new_keys: bfloat16 [32, 2048, 256], P('blk', 'group'), may hold values from -15 to 15
- new_values: bfloat16 [32, 2048, 256], P('blk', 'group'), may hold values from -4 to 4
- key_cache: bfloat16 [1280, 128, 256], P('blk', 'group'), may hold values from -4 to 4
- value_cache: bfloat16 [1280, 128, 256], P('blk', 'group'), may hold values from -4 to 4
- out_weight: bfloat16 [2560, 2560], replicated, may hold values from -0.375 to 0.375
- lengths: int32 [32], replicated, may hold values from 0 to 30720, as said below
- page_table: int32 [32, 32], replicated, may hold values from 0 to 1279, as said below
Outputs:
- hidden_states: bfloat16 [32, 2048, 2560], P('blk', 'group')
- key_cache_out: bfloat16 [1280, 128, 256], P('blk', 'group')
- value_cache_out: bfloat16 [1280, 128, 256], P('blk', 'group')
Inputs may be any that keep to these rules, and one draw needn't show every extreme that they name: `lengths`: multiples of 2048; some request has length 0 and some has 30720. `page_table`: all entries differ; page p lies on blk index p // 40; columns below 16 hold the request's last 16 pages before its group in order (pages that hold no part of a request where its length is short), the others the pages of its group in order; of one request's first 16 entries at most 1 lie on one blk index, of its last 16 at most 1, and both bounds are reached for every request.
All inputs are finite; a program needn't handle non-finite values.
Results may differ from a plain program's by a relative error of at most 0.009.
Values may be sent and summed in bfloat16 or wider, within the bound.
A program may use at most 256 MiB of HBM per device.

v0:
```python
import jax
import jax.numpy as jnp
from jax import lax
from jax.sharding import PartitionSpec as P

masked_score = -1e30
key_block_size = 512


def rotate(values, positions):
    quarter = values.shape[-1] // 4
    freq_table = 10000.0 ** (-jnp.arange(quarter, dtype=jnp.float32) / quarter)
    angles = positions.astype(jnp.float32)[..., None] * freq_table
    cosine = jnp.cos(angles)
    sine_part = jnp.sin(angles)
    leading = values[..., :quarter]
    trailing = values[..., quarter : 2 * quarter]
    return jnp.concatenate(
        [
            leading * cosine - trailing * sine_part,
            trailing * cosine + leading * sine_part,
            values[..., 2 * quarter :],
        ],
        axis=-1,
    )


def attend_block(carried, query_block, key_rows, value_rows, visible, score_scale):
    running_max, running_sum, running_acc = carried
    scores = (
        jnp.einsum("thd,kd->thk", query_block, key_rows, preferred_element_type=jnp.float32)
        * score_scale
    )
    scores = jnp.where(visible, scores, masked_score)
    new_max = jnp.maximum(running_max, jnp.max(scores, axis=2))
    weights = jnp.where(visible, jnp.exp(scores - new_max[:, :, None]), 0.0)
    factor = jnp.exp(running_max - new_max)
    new_sum = running_sum * factor + jnp.sum(weights, axis=2)
    new_acc = running_acc * factor[:, :, None] + jnp.einsum(
        "thk,kd->thd", weights.astype(jnp.bfloat16), value_rows, preferred_element_type=jnp.float32
    )
    return (new_max, new_sum, new_acc)


def attend(carried, query_block, key_rows, value_rows, visible, score_scale):
    key_total = key_rows.shape[0]
    for block_start in range(0, key_total, key_block_size):
        block_stop = min(block_start + key_block_size, key_total)
        carried = attend_block(
            carried,
            query_block,
            key_rows[block_start:block_stop],
            value_rows[block_start:block_stop],
            visible[:, :, block_start:block_stop],
            score_scale,
        )
    return carried


def body(queries, new_keys, new_values, key_cache, value_cache, out_weight, lengths, page_table):
    blk_count = lax.axis_size("blk")
    blk_index = lax.axis_index("blk")
    group_count = lax.axis_size("group")
    group_index = lax.axis_index("group")
    tok_rows = queries.shape[1]
    head_dim = new_keys.shape[2]
    head_count = queries.shape[2] // head_dim
    pages_here = key_cache.shape[0]
    page_rows = key_cache.shape[1]
    page_len = page_rows * group_count
    slot_count = page_table.shape[1]
    group_len = tok_rows * group_count
    fresh_pages = group_len // page_len
    window_pages = slot_count - fresh_pages
    window_len = window_pages * page_len
    score_scale = head_dim ** (-0.5)
    length = lengths[blk_index]
    my_table = page_table[blk_index]
    offsets = group_index * tok_rows + jnp.arange(tok_rows, dtype=jnp.int32)
    positions = length + offsets
    roped_queries = rotate(
        queries[0].astype(jnp.float32).reshape(tok_rows, head_count, head_dim), positions[:, None]
    ).astype(jnp.bfloat16)
    roped_keys = rotate(new_keys[0].astype(jnp.float32), positions).astype(jnp.bfloat16)
    all_keys, all_values = (
        lax.all_gather(roped_keys, "group", axis=0, tiled=True),
        lax.all_gather(new_values[0], "group", axis=0, tiled=True),
    )
    key_index = jnp.arange(group_len, dtype=jnp.int32)
    fresh_visible = key_index[None, :] <= offsets[:, None]
    initial = (
        jnp.full((tok_rows, head_count), masked_score, jnp.float32),
        jnp.zeros((tok_rows, head_count), jnp.float32),
        jnp.zeros((tok_rows, head_count, head_dim), jnp.float32),
    )
    carried = attend(
        initial, roped_queries, all_keys, all_values, fresh_visible[:, None, :], score_scale
    )
    old_table = my_table[:window_pages]
    blank_pages = jnp.zeros((window_pages, page_rows, head_dim), jnp.bfloat16)
    pieces = (
        lax.all_gather(key_cache, "blk", axis=0, tiled=True),
        lax.all_gather(value_cache, "blk", axis=0, tiled=True),
    )
    held_pages = pieces[0].shape[0]
    inside = (old_table >= 0) & (old_table < held_pages)
    clipped = jnp.clip(old_table, 0, held_pages - 1)
    old_keys = jnp.where(inside[:, None, None], pieces[0][clipped], blank_pages)
    old_values = jnp.where(inside[:, None, None], pieces[1][clipped], blank_pages)
    pieces = (
        lax.all_gather(old_keys, "group", axis=1, tiled=True),
        lax.all_gather(old_values, "group", axis=1, tiled=True),
    )
    piece_rows = pieces[0].shape[1]
    key_rows = pieces[0].reshape(-1, head_dim)
    value_rows = pieces[1].reshape(-1, head_dim)
    in_window = (
        jnp.arange(window_pages, dtype=jnp.int32)[:, None] * page_len
        + jnp.arange(piece_rows, dtype=jnp.int32)[None, :]
    ).reshape(-1)
    visible = (in_window[None, :] > offsets[:, None]) & (
        length - window_len + in_window[None, :] >= 0
    )
    carried = attend(carried, roped_queries, key_rows, value_rows, visible[:, None, :], score_scale)
    running_max, running_sum, running_acc = carried
    attended = (
        (running_acc / running_sum[:, :, None])
        .astype(jnp.bfloat16)
        .reshape(tok_rows, head_count * head_dim)
    )
    hidden = jnp.dot(attended, out_weight, preferred_element_type=jnp.float32).astype(jnp.bfloat16)[
        None
    ]
    cap_new = (fresh_pages + blk_count - 1) // blk_count
    quarter_keys = lax.dynamic_index_in_dim(
        all_keys.reshape(fresh_pages, group_count, page_rows, head_dim),
        group_index,
        axis=1,
        keepdims=False,
    )
    quarter_values = lax.dynamic_index_in_dim(
        all_values.reshape(fresh_pages, group_count, page_rows, head_dim),
        group_index,
        axis=1,
        keepdims=False,
    )
    new_owner = my_table[window_pages:] // pages_here
    fresh_ids = jnp.arange(fresh_pages, dtype=jnp.int32)
    before = fresh_ids[None, :] < fresh_ids[:, None]
    new_rank = jnp.sum(
        (before & (new_owner[None, :] == new_owner[:, None])).astype(jnp.int32), axis=1
    )
    placing = (
        (new_owner[None, None, :] == jnp.arange(blk_count, dtype=jnp.int32)[:, None, None])
        & (new_rank[None, None, :] == jnp.arange(cap_new, dtype=jnp.int32)[None, :, None])
    ).astype(jnp.bfloat16)
    send_new_keys = jnp.einsum(
        "ocj,jrd->ocrd", placing, quarter_keys, preferred_element_type=jnp.float32
    ).astype(jnp.bfloat16)
    send_new_values = jnp.einsum(
        "ocj,jrd->ocrd", placing, quarter_values, preferred_element_type=jnp.float32
    ).astype(jnp.bfloat16)
    arrived_keys, arrived_values = (
        lax.all_to_all(send_new_keys, "blk", split_axis=0, concat_axis=0, tiled=True),
        lax.all_to_all(send_new_values, "blk", split_axis=0, concat_axis=0, tiled=True),
    )
    owned_slots = page_table[:, window_pages:] // pages_here == blk_index
    hit_rank = jnp.cumsum(owned_slots.astype(jnp.int32), axis=1) - 1
    choose = owned_slots[:, None, :] & (
        hit_rank[:, None, :] == jnp.arange(cap_new, dtype=jnp.int32)[None, :, None]
    )
    target = jnp.where(
        jnp.any(choose, axis=2),
        jnp.sum(jnp.where(choose, page_table[:, None, window_pages:] % pages_here, 0), axis=2),
        pages_here,
    )
    key_out = key_cache.at[target.reshape(-1)].set(
        arrived_keys.reshape(-1, page_rows, head_dim), mode="drop"
    )
    value_out = value_cache.at[target.reshape(-1)].set(
        arrived_values.reshape(-1, page_rows, head_dim), mode="drop"
    )
    return (hidden, key_out, value_out)


def solution(mesh):
    return jax.shard_map(
        body,
        mesh=mesh,
        in_specs=(
            P("blk", "group", None),
            P("blk", "group", None),
            P("blk", "group", None),
            P("blk", "group", None),
            P("blk", "group", None),
            P(),
            P(),
            P(),
        ),
        out_specs=(P("blk", "group", None), P("blk", "group", None), P("blk", "group", None)),
        check_vma=False,
    )
```

profile of v0, /device:TPU:0, one launch (start us, length us, event | category | flops | bytes accessed | tf_op | source)
XLA Modules:
  0.0 1177.1 jit_solution(8598591531830800221)
XLA Ops:
  46.5 9.4 all-to-all-start
  56.2 11.0 all-gather.18.cloned.1.call-done
  72.0 7.3 fusion.3
  79.3 437.6 %all-gather.10.cloned.1.call-done = bf16[1280,32,256]{2,1,0:T(8,128)(2,1)} async-done(((bf16[40,32,256]{2,1,0:T(8,128)(2,1)}), bf16[1280,32,256]{2,1,0:T(8,128)(2,1)}) %all-gather.10.cloned.1.call-update) | async-done | bytes 20971536 | tf_op jit(solution)/shard_map/all_gather | solution.py:102
  517.0 7.5 gather_fusion
  524.5 443.7 %all-gather.14.cloned.1.call-done = bf16[1280,32,256]{2,1,0:T(8,128)(2,1)} async-done(((bf16[40,32,256]{2,1,0:T(8,128)(2,1)}), bf16[1280,32,256]{2,1,0:T(8,128)(2,1)}) %all-gather.14.cloned.1.call-update) | async-done | bytes 20971536 | tf_op jit(solution)/shard_map/all_gather | solution.py:103
  968.2 7.5 gather_fusion.1
  976.7 7.5 fusion.2
  984.2 7.3 fusion.1
  991.5 10.9 all-to-all-start.1
  1002.4 7.4 fusion
  1017.9 7.4 fusion.4
  1025.4 5.8 fusion.5
  1031.2 5.8 fusion.6
  1047.2 10.0 fusion.24
  1057.2 7.1 fusion.20
  1064.3 9.8 fusion.26
  1077.2 10.1 fusion.28
  1090.4 9.8 fusion.30
  1106.5 7.6 fusion.12
  1119.0 5.6 fusion.32
  1124.6 9.5 fusion.34
  1138.9 19.2 %divide_convert_fusion = bf16[512,10,256]{0,2,1:T(8,128)(2,1)} fusion(f32[512,10,256]{0,2,1:T(8,128)} %fusion.24, f32[512,10,256]{0,2,1:T(8,128)} %fusion.26, f32[512,10,256]{0,2,1:T(8,128)} %fusion.28, f32[512,10,256]{0,2,1:T(8,128)} %fusion.30, f32[512,10,256]{0,2,1:T(8,128)} %fusion.32, f32[512,10,256]{0,2,1:T(8,128)} %fusion.34, ...), kind=kOutput, calls=%fused_computation.52 | convolution fusion | flops 1377566720 | bytes 50536448 | tf_op jit(solution)/shard_map/thk,kd->thd/dot_general | solution.py:39
  1158.1 12.0 %fusion.80 = bf16[1,512,2560]{2,1,0:T(8,128)(2,1)} fusion(bf16[512,2560]{0,1:T(8,128)(2,1)} %bitcast.170, bf16[2560,2560]{1,0:T(8,128)(2,1)} %param.13), kind=kOutput, calls=%fused_computation.96 | convolution fusion | flops 6712197120 | bytes 18350080 | tf_op jit(solution)/shard_map/dot_general | solution.py:131
  (169 shorter events, 84.7 us)
Async XLA Ops:
  7.2 36.8 %all-gather.8.cloned.1.call-start = ((), (), s32[]{:S(2)}) async-start(), calls=%async_computation.2 | async-start | bytes 1310720 | tf_op jit(solution)/shard_map/all_gather | solution.py:86
  17.0 50.3 %all-gather.18.cloned.1.call-start = ((), (), s32[]{:S(2)}) async-start(), calls=%async_computation.7 | async-start | bytes 1310720 | tf_op jit(solution)/shard_map/all_gather | solution.py:87
  18.9 498.1 %all-gather.10.cloned.1.call-start = ((), (), s32[]{:S(2)}) async-start(), calls=%async_computation.3 | async-start | bytes 21626880 | tf_op jit(solution)/shard_map/all_gather | solution.py:102
  19.6 948.6 %all-gather.14.cloned.1.call-start = ((), (), s32[]{:S(2)}) async-start(), calls=%async_computation.5 | async-start | bytes 21626880 | tf_op jit(solution)/shard_map/all_gather | solution.py:103
  39.3 944.9 %copy-start.5 = (bf16[512,10,256]{2,0,1:T(8,128)(2,1)}, bf16[512,10,256]{2,0,1:T(8,128)(2,1)S(1)}, u32[]{:S(2)}) copy-start(bf16[512,10,256]{2,0,1:T(8,128)(2,1)S(1)} %pad_maximum_fusion) | copy-start | bytes 7864324
  42.8 36.5 %copy-start.11 = (pred[512,512]{0,1:T(8,128)(4,1)}, pred[512,512]{0,1:T(8,128)(4,1)S(1)}, u32[]{:S(2)}) copy-start(pred[512,512]{0,1:T(8,128)(4,1)S(1)} %get-tuple-element.31) | copy-start | bytes 786436
  46.5 945.1 %all-to-all-start = ((bf16[32,1,32,256]{3,2,1,0:T(8,128)(2,1)}), bf16[32,1,32,256]{3,2,1,0:T(8,128)(2,1)}, u32[]{:S(2)}, u32[]{:S(2)}) async-start(bf16[32,1,32,256]{3,2,1,0:T(8,128)(2,1)} %copy.87), calls=%async_computation | async-start | bytes 1048576 | tf_op jit(solution)/shard_map/all_to_all | solution.py:164
  55.9 960.5 %all-gather.12.cloned.1.call-start = ((), (), s32[]{:S(2)}) async-start(), calls=%async_computation.4 | async-start | bytes 1310720 | tf_op jit(solution)/shard_map/all_gather | solution.py:111
  991.5 18.4 %copy-start.3 = (bf16[40,32,256]{2,1,0:T(8,128)(2,1)S(1)}, bf16[40,32,256]{2,1,0:T(8,128)(2,1)}, u32[]{:S(2)}) copy-start(bf16[40,32,256]{2,1,0:T(8,128)(2,1)} %copy.115) | copy-start | bytes 1966084
  991.5 22.7 %copy-start.1 = (bf16[40,32,256]{2,1,0:T(8,128)(2,1)S(1)}, bf16[40,32,256]{2,1,0:T(8,128)(2,1)}, u32[]{:S(2)}) copy-start(bf16[40,32,256]{2,1,0:T(8,128)(2,1)} %copy.116) | copy-start | bytes 1966084
  991.5 22.7 %all-to-all-start.1 = ((bf16[32,1,32,256]{3,2,1,0:T(8,128)(2,1)}), bf16[32,1,32,256]{3,2,1,0:T(8,128)(2,1)S(1)}, u32[]{:S(2)}, u32[]{:S(2)}) async-start(bf16[32,1,32,256]{3,2,1,0:T(8,128)(2,1)} %copy.90), calls=%async_computation.1 | async-start | bytes 1048576 | tf_op jit(solution)/shard_map/all_to_all | solution.py:165
  1002.4 43.6 %all-gather.16.cloned.1.call-start = ((), (), s32[]{:S(2)}) async-start(), calls=%async_computation.6 | async-start | bytes 1310720 | tf_op jit(solution)/shard_map/all_gather | solution.py:112
  1009.9 29.0 %copy-start.25 = (f32[512,10]{0,1:T(8,128)}, f32[512,10]{0,1:T(8,128)S(1)}, u32[]{:S(2)}) copy-start(f32[512,10]{0,1:T(8,128)S(1)} %get-tuple-element.66) | copy-start | bytes 61444
  1039.7 24.6 %copy-start.21 = (f32[512,10]{0,1:T(8,128)}, f32[512,10]{0,1:T(8,128)S(1)}, u32[]{:S(2)}) copy-start(f32[512,10]{0,1:T(8,128)S(1)} %get-tuple-element.18) | copy-start | bytes 61444
  1039.7 37.5 %copy-start.22 = (f32[512,10]{0,1:T(8,128)}, f32[512,10]{0,1:T(8,128)S(1)}, u32[]{:S(2)}) copy-start(f32[512,10]{0,1:T(8,128)S(1)} %get-tuple-element.19) | copy-start | bytes 61444
  1039.7 50.7 %copy-start.23 = (f32[512,10]{0,1:T(8,128)}, f32[512,10]{0,1:T(8,128)S(1)}, u32[]{:S(2)}) copy-start(f32[512,10]{0,1:T(8,128)S(1)} %get-tuple-element.20) | copy-start | bytes 61444
  1039.7 60.6 %copy-start.24 = (f32[512,10]{0,1:T(8,128)}, f32[512,10]{0,1:T(8,128)S(1)}, u32[]{:S(2)}) copy-start(f32[512,10]{0,1:T(8,128)S(1)} %get-tuple-element.45) | copy-start | bytes 61444
  1039.7 63.7 %copy-start.19 = (f32[512,10]{0,1:T(8,128)}, f32[512,10]{0,1:T(8,128)S(1)}, u32[]{:S(2)}) copy-start(f32[512,10]{0,1:T(8,128)S(1)} %get-tuple-element.21) | copy-start | bytes 61444
  1047.2 26.9 %slice-start.12 = ((s8[10485760]{0:T(1024)(128)(4,1)}), s8[4194304]{0:T(1024)(128)(4,1)S(1)}, s32[]{:S(2)}) async-start(s8[10485760]{0:T(1024)(128)(4,1)} %bitcast.155), calls=%async_computation.20 | async-start | bytes 8388608
  1047.2 26.9 %slice-start.13 = ((s8[10485760]{0:T(1024)(128)(4,1)}), s8[4194304]{0:T(1024)(128)(4,1)S(1)}, s32[]{:S(2)}) async-start(s8[10485760]{0:T(1024)(128)(4,1)} %bitcast.155), calls=%async_computation.21 | async-start | bytes 8388608
  1064.3 23.0 %slice-start.9 = ((s8[10485760]{0:T(1024)(128)(4,1)}), s8[4194304]{0:T(1024)(128)(4,1)S(1)}, s32[]{:S(2)}) async-start(s8[10485760]{0:T(1024)(128)(4,1)} %bitcast.153), calls=%async_computation.17 | async-start | bytes 8388608
  1064.3 23.0 %slice-start.10 = ((s8[10485760]{0:T(1024)(128)(4,1)}), s8[4194304]{0:T(1024)(128)(4,1)S(1)}, s32[]{:S(2)}) async-start(s8[10485760]{0:T(1024)(128)(4,1)} %bitcast.153), calls=%async_computation.18 | async-start | bytes 8388608
  1077.2 23.0 %slice-start.6 = ((s8[10485760]{0:T(1024)(128)(4,1)}), s8[4194304]{0:T(1024)(128)(4,1)S(1)}, s32[]{:S(2)}) async-start(s8[10485760]{0:T(1024)(128)(4,1)} %bitcast.151), calls=%async_computation.14 | async-start | bytes 8388608
  1077.2 23.0 %slice-start.7 = ((s8[10485760]{0:T(1024)(128)(4,1)}), s8[4194304]{0:T(1024)(128)(4,1)S(1)}, s32[]{:S(2)}) async-start(s8[10485760]{0:T(1024)(128)(4,1)} %bitcast.151), calls=%async_computation.15 | async-start | bytes 8388608
  (29 other events, 269.7 us)
Sparse Core Ops, SparseCore 0:
  17.1 23.2 all-gather.7
  42.1 25.1 all-gather.17
  69.5 447.4 all-gather.9
  518.5 449.7 all-gather.13
  976.8 23.0 all-gather.11
  1016.5 19.6 all-gather.15
where the time goes:
time: 1180 us
  waiting for transfers between devices  895 us (76%)
  matrix products  142 us (12%)
  other arithmetic  52.3 us (4%)
  local copies, waits for them, and re-layouts  51.9 us (4%)
  starting transfers between devices  20.8 us (2%)
  between operations  15.4 us (1%)
    all_gather x1, waiting for transfers between devices, body(): lax.all_gather(value_cache, 'blk', axis=0, tiled=True)  444 us
    all_gather x1, waiting for transfers between devices, body(): lax.all_gather(key_cache, 'blk', axis=0, tiled=True)  438 us
    dot_general x8, matrix products, attend_block(): jnp.einsum('thk,kd->thd', weights.astype(jnp.bfloat16), value_rows, prefe...  78.7 us
    dot_general x8, matrix products, attend_block(): jnp.einsum('thd,kd->thk', query_block, key_rows, preferred_element_type=j...  50.4 us
    reduce_sum x8, other arithmetic, attend_block(): new_sum = running_sum * factor + jnp.sum(weights, axis=2)  33.2 us
  transfers between devices with their start and end apart: 8, of which 4 were waited for; matrix products, arithmetic and copies ran while one was open for 9% of the time, Pallas kernels for 0%

commit v1 on v0

--- a/solution.py
+++ b/solution.py
@@ -1,3 +1,4 @@
+import functools
 import jax
 import jax.numpy as jnp
 from jax import lax
@@ -5,6 +6,16 @@
 
 masked_score = -1e30
 key_block_size = 512
+
+
+def list_leaf(z, which_axis, axis_no):
+    return jnp.concatenate(
+        lax.all_to_all(jnp.stack(lax.axis_size(which_axis) * [z], axis=0), which_axis, 0, 0),
+        axis=axis_no,
+    )
+
+
+_scan_stages_all = functools.partial(list_leaf, which_axis="blk", axis_no=0)
 
 
 def rotate(values, positions):
@@ -98,10 +109,7 @@
     )
     old_table = my_table[:window_pages]
     blank_pages = jnp.zeros((window_pages, page_rows, head_dim), jnp.bfloat16)
-    pieces = (
-        lax.all_gather(key_cache, "blk", axis=0, tiled=True),
-        lax.all_gather(value_cache, "blk", axis=0, tiled=True),
-    )
+    pieces = (_scan_stages_all(key_cache), lax.all_gather(value_cache, "blk", axis=0, tiled=True))
     held_pages = pieces[0].shape[0]
     inside = (old_table >= 0) & (old_table < held_pages)
     clipped = jnp.clip(old_table, 0, held_pages - 1)

time: 1180 us -> 988 us (0.84)
  waiting for transfers between devices: 895 us -> 685 us
    all_gather x1 -> x0, waiting for transfers between devices: 438 us -> none  [body(): lax.all_gather(key_cache, 'blk', axis=0, tiled=True)]
    all_to_all x0 -> x1, waiting for transfers between devices: none -> 315 us  [list_leaf(): lax.all_to_all(jnp.stack(lax.axis_size(which_axis) * [z], axis=0), which_...]
    all_gather x1, waiting for transfers between devices: 444 us -> 335 us  [body(): lax.all_gather(value_cache, 'blk', axis=0, tiled=True)]
    all_gather x1, waiting for transfers between devices: 11 us -> 33.1 us  [body(): lax.all_gather(new_values[0], 'group', axis=0, tiled=True)]
  transfers between devices with their start and end apart: 8 -> 8, of which waited for: 4 -> 4; matrix products, arithmetic and copies ran while one was open for 9% -> 12% of each run, Pallas kernels for 0% -> 0%
where the time goes in v1:
time: 988 us; the launch traced here: 980 us
  waiting for transfers between devices  685 us (69%)
  matrix products  138 us (14%)
  other arithmetic  56.7 us (6%)
  local copies, waits for them, and re-layouts  54 us (5%)
  starting transfers between devices  30.6 us (3%)
  between operations  15.2 us (2%)
    all_gather x1, waiting for transfers between devices, body(): lax.all_gather(value_cache, 'blk', axis=0, tiled=True)  335 us
    all_to_all x1, waiting for transfers between devices, list_leaf(): lax.all_to_all(jnp.stack(lax.axis_size(which_axis) * [z], axis=0), which_...  315 us
    dot_general x8, matrix products, attend_block(): jnp.einsum('thk,kd->thd', weights.astype(jnp.bfloat16), value_rows, prefe...  73.8 us
    dot_general x8, matrix products, attend_block(): jnp.einsum('thd,kd->thk', query_block, key_rows, preferred_element_type=j...  51.2 us
    all_gather x1, waiting for transfers between devices, body(): lax.all_gather(new_values[0], 'group', axis=0, tiled=True)  33.1 us
    reduce_sum x8, other arithmetic, attend_block(): new_sum = running_sum * factor + jnp.sum(weights, axis=2)  33 us
  transfers between devices with their start and end apart: 8, of which 4 were waited for; matrix products, arithmetic and copies ran while one was open for 12% of the time, Pallas kernels for 0%

profile of v1, /device:TPU:0, one launch (start us, length us, event | category | flops | bytes accessed | tf_op | source)
XLA Modules:
  0.0 979.6 jit_solution(4560461428958498633)
XLA Ops:
  20.0 7.4 stack.2
  27.4 9.7 all-to-all-start
  64.0 33.1 %all-gather.15.cloned.1.call-done = bf16[1,2048,256]{1,2,0:T(8,128)(2,1)} async-done(((bf16[1,512,256]{1,2,0:T(8,128)(2,1)}), bf16[1,2048,256]{1,2,0:T(8,128)(2,1)}) %all-gather.15.cloned.1.call-update) | async-done | bytes 1048592 | tf_op jit(solution)/shard_map/all_gather | solution.py:98
  101.9 7.3 fusion.3
  109.2 315.3 %all-to-all-done = bf16[32,40,32,256]{3,2,1,0:T(8,128)(2,1)} async-done(((bf16[32,40,32,256]{3,2,1,0:T(8,128)(2,1)}), bf16[32,40,32,256]{3,2,1,0:T(8,128)(2,1)}, u32[]{:S(2)}, u32[]{:S(2)}) %all-to-all-start) | async-done | bytes 20971552 | tf_op jit(solution)/shard_map/all_to_all | solution.py:13
  424.5 16.3 %all-to-all-start.1 = ((bf16[32,1,32,256]{3,2,1,0:T(8,128)(2,1)}), bf16[32,1,32,256]{3,2,1,0:T(8,128)(2,1)}, u32[]{:S(2)}, u32[]{:S(2)}) async-start(bf16[32,1,32,256]{3,2,1,0:T(8,128)(2,1)} %copy.87), calls=%async_computation.1 | async-start | bytes 1048576 | tf_op jit(solution)/shard_map/all_to_all | solution.py:172
  441.3 7.5 gather_fusion
  448.8 335.2 %all-gather.11.cloned.1.call-done = bf16[1280,32,256]{2,1,0:T(8,128)(2,1)} async-done(((bf16[40,32,256]{2,1,0:T(8,128)(2,1)}), bf16[1280,32,256]{2,1,0:T(8,128)(2,1)}) %all-gather.11.cloned.1.call-update) | async-done | bytes 20971536 | tf_op jit(solution)/shard_map/all_gather | solution.py:112
  784.0 8.2 gather_fusion.1
  794.1 7.5 fusion.2
  801.6 7.3 fusion.1
  813.0 7.4 fusion
  831.9 6.3 fusion.4
  838.2 5.9 fusion.6
  844.1 5.9 fusion.5
  855.2 10.3 %fusion.24 = f32[512,10,256]{0,2,1:T(8,128)} fusion(bf16[512,256,1]{1,0,2:T(8,128)(2,1)S(1)} %bitcast.169, f32[512,10,512]{0,2,1:T(8,128)} %copy-done, f32[512,10]{0,1:T(8,128)S(1)} %get-tuple-element.17, pred[512,512]{0,1:T(8,128)(4,1)S(1)} %copy-done.18), kind=kOutput, calls=%fused_computation.44 | convolution fusion | flops 1355284480 | bytes 16273408 | tf_op jit(solution)/shard_map/thk,kd->thd/dot_general | solution.py:50
  873.2 7.1 fusion.18
  880.3 9.8 %fusion.28 = f32[512,10,256]{0,2,1:T(8,128)} fusion(bf16[512,256,1]{1,0,2:T(8,128)(2,1)S(1)} %bitcast.164, f32[512,10,512]{0,2,1:T(8,128)} %get-tuple-element.57, f32[512,10]{0,1:T(8,128)S(1)} %get-tuple-element.19, pred[512,512]{0,1:T(8,128)(4,1)S(1)} %copy-done.16), kind=kOutput, calls=%fused_computation.46 | convolution fusion | flops 1355284480 | bytes 16273408 | tf_op jit(solution)/shard_map/thk,kd->thd/dot_general | solution.py:50
  893.3 9.9 %fusion.30 = f32[512,10,256]{0,2,1:T(8,128)} fusion(bf16[512,256,1]{1,0,2:T(8,128)(2,1)S(1)} %bitcast.162, f32[512,10,512]{0,2,1:T(8,128)} %get-tuple-element.59, f32[512,10]{0,1:T(8,128)S(1)} %get-tuple-element.20, pred[512,512]{0,1:T(8,128)(4,1)S(1)} %copy-done.15), kind=kOutput, calls=%fused_computation.47 | convolution fusion | flops 1355284480 | bytes 16273408 | tf_op jit(solution)/shard_map/thk,kd->thd/dot_general | solution.py:50
  909.6 7.2 fusion.12
  921.7 5.9 fusion.32
  927.6 9.6 fusion.34
  941.9 19.0 %divide_convert_fusion = bf16[512,10,256]{0,2,1:T(8,128)(2,1)} fusion(f32[512,10,256]{0,2,1:T(8,128)} %fusion.24, f32[512,10,256]{0,2,1:T(8,128)} %fusion.26, f32[512,10,256]{0,2,1:T(8,128)} %fusion.28, f32[512,10,256]{0,2,1:T(8,128)} %fusion.30, f32[512,10,256]{0,2,1:T(8,128)} %fusion.32, f32[512,10,256]{0,2,1:T(8,128)} %fusion.34, ...), kind=kOutput, calls=%fused_computation.52 | convolution fusion | flops 1377566720 | bytes 50536448 | tf_op jit(solution)/shard_map/thk,kd->thd/dot_general | solution.py:50
  960.9 12.0 %fusion.80 = bf16[1,512,2560]{2,1,0:T(8,128)(2,1)} fusion(bf16[512,2560]{0,1:T(8,128)(2,1)} %bitcast.171, bf16[2560,2560]{1,0:T(8,128)(2,1)} %param.13), kind=kOutput, calls=%fused_computation.96 | convolution fusion | flops 6712197120 | bytes 18350080 | tf_op jit(solution)/shard_map/dot_general | solution.py:139
  (175 shorter events, 93.6 us)
Async XLA Ops:
  7.2 54.4 %all-gather.7.cloned.1.call-start = ((), (), s32[]{:S(2)}) async-start(), calls=%async_computation.3 | async-start | bytes 1310720 | tf_op jit(solution)/shard_map/all_gather | solution.py:97
  17.4 79.7 %all-gather.15.cloned.1.call-start = ((), (), s32[]{:S(2)}) async-start(), calls=%async_computation.7 | async-start | bytes 1310720 | tf_op jit(solution)/shard_map/all_gather | solution.py:98
  19.3 764.7 %all-gather.11.cloned.1.call-start = ((), (), s32[]{:S(2)}) async-start(), calls=%async_computation.5 | async-start | bytes 21626880 | tf_op jit(solution)/shard_map/all_gather | solution.py:112
  27.4 397.1 %all-to-all-start = ((bf16[32,40,32,256]{3,2,1,0:T(8,128)(2,1)}), bf16[32,40,32,256]{3,2,1,0:T(8,128)(2,1)}, u32[]{:S(2)}, u32[]{:S(2)}) async-start(bf16[32,40,32,256]{3,2,1,0:T(8,128)(2,1)} %stack.2), calls=%async_computation | async-start | bytes 41943040 | tf_op jit(solution)/shard_map/all_to_all | solution.py:13
  55.7 745.9 %copy-start.4 = (bf16[512,10,256]{2,0,1:T(8,128)(2,1)}, bf16[512,10,256]{2,0,1:T(8,128)(2,1)S(1)}, u32[]{:S(2)}) copy-start(bf16[512,10,256]{2,0,1:T(8,128)(2,1)S(1)} %pad_maximum_fusion) | copy-start | bytes 7864324
  60.4 48.8 %copy-start.12 = (pred[512,512]{0,1:T(8,128)(4,1)}, pred[512,512]{0,1:T(8,128)(4,1)S(1)}, u32[]{:S(2)}) copy-start(pred[512,512]{0,1:T(8,128)(4,1)S(1)} %get-tuple-element.31) | copy-start | bytes 786436
  424.5 384.5 %all-to-all-start.1 = ((bf16[32,1,32,256]{3,2,1,0:T(8,128)(2,1)}), bf16[32,1,32,256]{3,2,1,0:T(8,128)(2,1)}, u32[]{:S(2)}, u32[]{:S(2)}) async-start(bf16[32,1,32,256]{3,2,1,0:T(8,128)(2,1)} %copy.87), calls=%async_computation.1 | async-start | bytes 1048576 | tf_op jit(solution)/shard_map/all_to_all | solution.py:172
  440.8 385.9 %all-gather.9.cloned.1.call-start = ((), (), s32[]{:S(2)}) async-start(), calls=%async_computation.4 | async-start | bytes 1310720 | tf_op jit(solution)/shard_map/all_gather | solution.py:119
  808.9 16.0 %copy-start.1 = (bf16[40,32,256]{2,1,0:T(8,128)(2,1)S(1)}, bf16[40,32,256]{2,1,0:T(8,128)(2,1)}, u32[]{:S(2)}) copy-start(bf16[40,32,256]{2,1,0:T(8,128)(2,1)} %copy.116) | copy-start | bytes 1966084
  808.9 16.0 %all-to-all-start.2 = ((bf16[32,1,32,256]{3,2,1,0:T(8,128)(2,1)}), bf16[32,1,32,256]{3,2,1,0:T(8,128)(2,1)S(1)}, u32[]{:S(2)}, u32[]{:S(2)}) async-start(bf16[32,1,32,256]{3,2,1,0:T(8,128)(2,1)} %copy.90), calls=%async_computation.2 | async-start | bytes 1048576 | tf_op jit(solution)/shard_map/all_to_all | solution.py:173
  813.0 15.3 %copy-start.18 = (pred[512,512]{0,1:T(8,128)(4,1)S(1)}, pred[512,512]{0,1:T(8,128)(4,1)}, u32[]{:S(2)}) copy-start(pred[512,512]{0,1:T(8,128)(4,1)} %get-tuple-element.35) | copy-start | bytes 786436
  813.0 40.8 %all-gather.13.cloned.1.call-start = ((), (), s32[]{:S(2)}) async-start(), calls=%async_computation.6 | async-start | bytes 1310720 | tf_op jit(solution)/shard_map/all_gather | solution.py:120
  820.5 29.5 %copy-start.26 = (f32[512,10]{0,1:T(8,128)}, f32[512,10]{0,1:T(8,128)S(1)}, u32[]{:S(2)}) copy-start(f32[512,10]{0,1:T(8,128)S(1)} %get-tuple-element.66) | copy-start | bytes 61444
  831.9 18.7 %copy-start = (f32[512,10,512]{0,2,1:T(8,128)}, f32[512,10,512]{0,2,1:T(8,128)S(1)}, u32[]{:S(2)}) copy-start(f32[512,10,512]{0,2,1:T(8,128)S(1)} %get-tuple-element.53) | copy-start | bytes 31457284
  850.6 14.8 %copy-start.21 = (f32[512,10]{0,1:T(8,128)}, f32[512,10]{0,1:T(8,128)S(1)}, u32[]{:S(2)}) copy-start(f32[512,10]{0,1:T(8,128)S(1)} %get-tuple-element.17) | copy-start | bytes 61444
  850.6 18.0 %copy-start.22 = (f32[512,10]{0,1:T(8,128)}, f32[512,10]{0,1:T(8,128)S(1)}, u32[]{:S(2)}) copy-start(f32[512,10]{0,1:T(8,128)S(1)} %get-tuple-element.18) | copy-start | bytes 61444
  850.6 29.7 %copy-start.23 = (f32[512,10]{0,1:T(8,128)}, f32[512,10]{0,1:T(8,128)S(1)}, u32[]{:S(2)}) copy-start(f32[512,10]{0,1:T(8,128)S(1)} %get-tuple-element.19) | copy-start | bytes 61444
  850.6 42.7 %copy-start.24 = (f32[512,10]{0,1:T(8,128)}, f32[512,10]{0,1:T(8,128)S(1)}, u32[]{:S(2)}) copy-start(f32[512,10]{0,1:T(8,128)S(1)} %get-tuple-element.20) | copy-start | bytes 61444
  850.6 52.6 %copy-start.25 = (f32[512,10]{0,1:T(8,128)}, f32[512,10]{0,1:T(8,128)S(1)}, u32[]{:S(2)}) copy-start(f32[512,10]{0,1:T(8,128)S(1)} %get-tuple-element.45) | copy-start | bytes 61444
  850.6 55.8 %copy-start.20 = (f32[512,10]{0,1:T(8,128)}, f32[512,10]{0,1:T(8,128)S(1)}, u32[]{:S(2)}) copy-start(f32[512,10]{0,1:T(8,128)S(1)} %get-tuple-element.21) | copy-start | bytes 61444
  868.6 21.6 %slice-start.9 = ((s8[10485760]{0:T(1024)(128)(4,1)}), s8[4194304]{0:T(1024)(128)(4,1)S(1)}, s32[]{:S(2)}) async-start(s8[10485760]{0:T(1024)(128)(4,1)} %bitcast.154), calls=%async_computation.17 | async-start | bytes 8388608
  868.6 21.6 %slice-start.10 = ((s8[10485760]{0:T(1024)(128)(4,1)}), s8[4194304]{0:T(1024)(128)(4,1)S(1)}, s32[]{:S(2)}) async-start(s8[10485760]{0:T(1024)(128)(4,1)} %bitcast.154), calls=%async_computation.18 | async-start | bytes 8388608
  880.3 22.9 %slice-start.6 = ((s8[10485760]{0:T(1024)(128)(4,1)}), s8[4194304]{0:T(1024)(128)(4,1)S(1)}, s32[]{:S(2)}) async-start(s8[10485760]{0:T(1024)(128)(4,1)} %bitcast.152), calls=%async_computation.14 | async-start | bytes 8388608
  880.3 22.9 %slice-start.7 = ((s8[10485760]{0:T(1024)(128)(4,1)}), s8[4194304]{0:T(1024)(128)(4,1)S(1)}, s32[]{:S(2)}) async-start(s8[10485760]{0:T(1024)(128)(4,1)} %bitcast.152), calls=%async_computation.15 | async-start | bytes 8388608
  (32 other events, 285.9 us)
Sparse Core Ops, SparseCore 0:
  17.5 23.2 all-gather.6
  42.5 54.6 all-gather.14
  99.3 684.5 all-gather.10
  794.2 16.8 all-gather.8
  826.8 21.0 all-gather.12
